TPU v7x, 32 devices: a whole 2x2x4 slice. The times are simulated.
32 devices in a mesh: dp: 8 (over y, x, core), tensor: 4 (over z).
Axes of the slice: x: 2, y: 2, z: 4, core: 2. Of those that a mesh axis runs over, the one named last changes fastest.
Arguments:
- send_order: int32 [32, 32], P(('dp', 'tensor')), may hold values from 0 to 31, each once within a row
- master: float32 [32, 32, 2048], P(('dp', 'tensor')), may hold values from -6 to 6
- first_code: bfloat16 [32, 32, 2048], P(('dp', 'tensor')), may hold values from -1 to 1
- first_scale: float32 [32, 32], P(('dp', 'tensor')), may hold values from 0.1 to 2
- second_code: bfloat16 [32, 32, 2048], P(('dp', 'tensor')), may hold values from 0.049804688 to 1
- second_scale: float32 [32, 32], P(('dp', 'tensor')), may hold values from 0.5 to 20
- grads: bfloat16 [8, 4, 8, 32, 2048], P('dp', 'tensor'), may hold values from -6 to 6
Outputs:
- new_master: float32 [32, 32, 2048], P(('dp', 'tensor'))
- new_first_code: bfloat16 [32, 32, 2048], P(('dp', 'tensor'))
- new_first_scale: float32 [32, 32], P(('dp', 'tensor'))
- new_second_code: bfloat16 [32, 32, 2048], P(('dp', 'tensor'))
- new_second_scale: float32 [32, 32], P(('dp', 'tensor'))
- weights: bfloat16 [4, 8, 32, 2048], P('tensor')
Inputs may be any that keep to these rules, and one draw needn't show every extreme that they name: `send_order`: each row is an ordering of the slots 0 to 31, each once.
All inputs are finite; a program needn't handle non-finite values. Where the computation divides by a largest or mean magnitude, that divisor is 1e-20 or more.
Results may differ from a plain program's by a relative error of at most 0.001.
Values may be sent and summed in bfloat16 or wider, within the bound.
A program may use at most 128 MiB of HBM per device.

v0:
```python
import jax
import jax.numpy as jnp
from jax import lax
from jax.sharding import PartitionSpec as P

STEP = 10


def on_device(send_order, master, first_code, first_scale, second_code, second_scale, grads):
    count_dp = lax.axis_size("dp")
    count_tensor = lax.axis_size("tensor")
    devices_all = count_dp * count_tensor
    slots = master.shape[1]
    width = master.shape[2]
    per_peer = slots // devices_all
    order_row = send_order[0]
    moved = (
        master[0][order_row],
        first_code[0][order_row],
        first_scale[0][order_row],
        second_code[0][order_row],
        second_scale[0][order_row],
    )
    shaped = tuple((item.reshape((devices_all, per_peer) + item.shape[1:]) for item in moved))
    arrived = (
        lax.all_to_all(shaped[0], ("dp", "tensor"), split_axis=0, concat_axis=0, tiled=True),
        lax.all_to_all(
            shaped[1].astype(jnp.float32), ("dp", "tensor"), split_axis=0, concat_axis=0, tiled=True
        ).astype(jnp.bfloat16),
        lax.all_to_all(shaped[2], ("dp", "tensor"), split_axis=0, concat_axis=0, tiled=True),
        lax.all_to_all(
            shaped[3].astype(jnp.float32), ("dp", "tensor"), split_axis=0, concat_axis=0, tiled=True
        ).astype(jnp.bfloat16),
        lax.all_to_all(shaped[4], ("dp", "tensor"), split_axis=0, concat_axis=0, tiled=True),
    )
    master_new = arrived[0].reshape(slots, width)
    code_one = arrived[1].reshape(slots, width)
    scale_one = arrived[2].reshape(slots)
    code_two = arrived[3].reshape(slots, width)
    scale_two = arrived[4].reshape(slots)
    summed = lax.psum_scatter(grads.astype(jnp.float32), "dp", scatter_dimension=2, tiled=True)
    grad = summed.reshape(slots, width)
    first = code_one.astype(jnp.float32) * scale_one[:, None]
    second = code_two.astype(jnp.float32) * scale_two[:, None]
    moment_one = 0.9 * first + 0.1 * grad
    moment_two = 0.95 * second + 0.05 * grad * grad
    corr_one = 1.0 - 0.9**STEP
    corr_two = 1.0 - 0.95**STEP
    update = moment_one / corr_one / (jnp.sqrt(moment_two / corr_two) + 1e-08) + 0.1 * master_new
    new_master = master_new - 0.01 * update
    new_scale_one = jnp.max(jnp.abs(moment_one), axis=1) + 1e-06
    new_code_one = (moment_one / new_scale_one[:, None]).astype(jnp.bfloat16)
    new_scale_two = jnp.max(jnp.abs(moment_two), axis=1) + 1e-06
    new_code_two = (moment_two / new_scale_two[:, None]).astype(jnp.bfloat16)
    local_weights = new_master.astype(jnp.bfloat16).reshape(1, 1, slots, width)
    weights = lax.all_gather(local_weights, "dp", axis=1, tiled=True)
    return (
        new_master.reshape(1, slots, width),
        new_code_one.reshape(1, slots, width),
        new_scale_one.reshape(1, slots),
        new_code_two.reshape(1, slots, width),
        new_scale_two.reshape(1, slots),
        weights,
    )


def solution(mesh):
    placed = (
        P(("dp", "tensor"), None),
        P(("dp", "tensor"), None, None),
        P(("dp", "tensor"), None, None),
        P(("dp", "tensor"), None),
        P(("dp", "tensor"), None, None),
        P(("dp", "tensor"), None),
        P("dp", "tensor", None, None, None),
    )
    return jax.shard_map(
        on_device,
        mesh=mesh,
        in_specs=placed,
        out_specs=(
            P(("dp", "tensor"), None, None),
            P(("dp", "tensor"), None, None),
            P(("dp", "tensor"), None),
            P(("dp", "tensor"), None, None),
            P(("dp", "tensor"), None),
            P("tensor", None, None, None),
        ),
        check_vma=False,
    )
```

profile of v0, /device:TPU:0, one launch (start us, length us, event | category | flops | bytes accessed | tf_op | source)
XLA Modules:
  0.0 104.7 jit_solution(7902596441690301470)
XLA Ops:
  7.2 2.9 %bitcast_convert_fusion = f32[1,1,8,32,2048]{4,3,1,0,2:T(8,128)} fusion(bf16[1,1,8,32,2048]{4,3,2,1,0:T(8,128)(2,1)} %param.13), kind=kLoop, calls=%fused_computation.5 | loop fusion | flops 524288 | bytes 3145728 | tf_op jit(solution)/shard_map/convert_element_type | solution.py:41
  10.2 0.7 gather_fusion.4
  10.9 0.7 copy.43
  11.6 7.3 %all-to-all-start.4 = ((f32[32,1,1]{2,1,0:T(1,128)}), f32[32,1,1]{2,1,0:T(1,128)S(1)}, u32[]{:S(2)}, u32[]{:S(2)}) async-start(f32[32,1,1]{2,1,0:T(1,128)} %copy.43), calls=%async_computation.5 | async-start | bytes 32768 | tf_op jit(solution)/shard_map/all_to_all | solution.py:34
  18.9 0.7 gather_fusion.3
  19.6 0.7 gather_fusion.2
  20.3 0.7 copy.40
  21.0 5.0 %all-to-all-done.4 = f32[32,1,1]{2,1,0:T(1,128)S(1)} async-done(((f32[32,1,1]{2,1,0:T(1,128)}), f32[32,1,1]{2,1,0:T(1,128)S(1)}, u32[]{:S(2)}, u32[]{:S(2)}) %all-to-all-start.4) | async-done | bytes 160 | tf_op jit(solution)/shard_map/all_to_all | solution.py:34
  26.0 2.5 %all-to-all-start.2 = ((f32[32,1,1]{2,1,0:T(1,128)}), f32[32,1,1]{2,1,0:T(1,128)S(1)}, u32[]{:S(2)}, u32[]{:S(2)}) async-start(f32[32,1,1]{2,1,0:T(1,128)} %copy.40), calls=%async_computation.2 | async-start | bytes 32768 | tf_op jit(solution)/shard_map/all_to_all | solution.py:30
  28.6 0.5 broadcast.345
  29.1 0.7 reduce.2
  29.8 0.7 reshape.649
  30.5 5.2 %all-to-all-done.2 = f32[32,1,1]{2,1,0:T(1,128)S(1)} async-done(((f32[32,1,1]{2,1,0:T(1,128)}), f32[32,1,1]{2,1,0:T(1,128)S(1)}, u32[]{:S(2)}, u32[]{:S(2)}) %all-to-all-start.2) | async-done | bytes 160 | tf_op jit(solution)/shard_map/all_to_all | solution.py:30
  35.7 2.6 %all-to-all-start.3 = ((bf16[32,2,1024]{2,1,0:T(2,128)(2,1)}), bf16[32,2,1024]{2,1,0:T(2,128)(2,1)S(1)}, u32[]{:S(2)}, u32[]{:S(2)}) async-start(bf16[32,2,1024]{2,1,0:T(2,128)(2,1)} %reshape.649), calls=%async_computation.4 | async-start | bytes 262144 | tf_op jit(solution)/shard_map/all_to_all | solution.py:31
  38.3 0.7 gather_fusion.1
  39.0 0.7 reduce.3
  39.6 0.7 reshape.647
  40.4 6.3 %all-to-all-done.3 = bf16[32,2,1024]{2,1,0:T(2,128)(2,1)S(1)} async-done(((bf16[32,2,1024]{2,1,0:T(2,128)(2,1)}), bf16[32,2,1024]{2,1,0:T(2,128)(2,1)S(1)}, u32[]{:S(2)}, u32[]{:S(2)}) %all-to-all-start.3) | async-done | bytes 131104 | tf_op jit(solution)/shard_map/all_to_all | solution.py:31
  46.7 2.6 %all-to-all-start.1 = ((bf16[32,2,1024]{2,1,0:T(2,128)(2,1)}), bf16[32,2,1024]{2,1,0:T(2,128)(2,1)S(1)}, u32[]{:S(2)}, u32[]{:S(2)}) async-start(bf16[32,2,1024]{2,1,0:T(2,128)(2,1)} %reshape.647), calls=%async_computation.1 | async-start | bytes 262144 | tf_op jit(solution)/shard_map/all_to_all | solution.py:27
  49.3 0.7 gather_fusion
  49.9 1.0 copy.37
  50.9 6.7 %all-to-all-done.1 = bf16[32,2,1024]{2,1,0:T(2,128)(2,1)S(1)} async-done(((bf16[32,2,1024]{2,1,0:T(2,128)(2,1)}), bf16[32,2,1024]{2,1,0:T(2,128)(2,1)S(1)}, u32[]{:S(2)}, u32[]{:S(2)}) %all-to-all-start.1) | async-done | bytes 131104 | tf_op jit(solution)/shard_map/all_to_all | solution.py:27
  57.6 2.6 %all-to-all-start = ((f32[32,1,2048]{2,1,0:T(1,128)}), f32[32,1,2048]{2,1,0:T(1,128)S(1)}, u32[]{:S(2)}, u32[]{:S(2)}) async-start(f32[32,1,2048]{2,1,0:T(1,128)} %copy.37), calls=%async_computation | async-start | bytes 524288 | tf_op jit(solution)/shard_map/all_to_all | solution.py:26
  60.3 0.3 reduce.1
  61.2 9.2 %all-to-all-done = f32[32,1,2048]{2,1,0:T(1,128)S(1)} async-done(((f32[32,1,2048]{2,1,0:T(1,128)}), f32[32,1,2048]{2,1,0:T(1,128)S(1)}, u32[]{:S(2)}, u32[]{:S(2)}) %all-to-all-start) | async-done | bytes 262176 | tf_op jit(solution)/shard_map/all_to_all | solution.py:26
  70.5 2.8 %fusion.24 = bf16[1,1,32,2048]{3,0,2,1:T(2,128)(2,1)S(1)} fusion(f32[1,1,1,32,2048]{4,3,1,0,2:T(8,128)} %reduce-scatter.2.cloned.1.call-done, f32[1,1,32,2048]{3,2,1,0:T(8,128)S(1)} %get-tuple-element.26, f32[32,1,2048]{2,1,0:T(1,128)S(1)} %all-to-all-done, f32[32]{0:T(128)S(1)} %reduce.1, bf16[32,1,2048]{2,1,0:T(2,128)(2,1)S(1)} %reshape.650), kind=kLoop, calls=%fused_computation.50 | loop fusion | flops 1114112 | bytes 1048704 | tf_op jit(solution)/shard_map/convert_element_type | solution.py:55
  73.3 0.7 copy.45
  74.3 0.3 fusion.3
  74.7 0.5 fusion.26
  75.2 1.2 %divide_convert_fusion = (bf16[1,32,2048]{2,1,0:T(8,128)(2,1)}, f32[1,32,2048]{2,1,0:T(8,128)}, bf16[1,32,2048]{2,1,0:T(8,128)(2,1)}) fusion(f32[32]{0:T(128)S(1)} %get-tuple-element.35, f32[1,1,1,32,2048]{4,3,1,0,2:T(8,128)S(1)} %copy-done.5, f32[32,1,2048]{2,1,0:T(1,128)S(1)} %convert_element_type.203, f32[32]{0:T(128)S(1)} %reduce.1, f32[32]{0:T(128)S(1)} %reduce, ...), kind=kLoop, calls=%fused_computation.47 | loop fusion | flops 1441792 | bytes 1442304 | tf_op jit(solution)/shard_map/convert_element_type | solution.py:54
  76.4 19.2 %all-gather.2.cloned.1.call-done = bf16[1,8,32,2048]{3,2,0,1:T(8,128)(2,1)} async-done(((bf16[1,1,32,2048]{3,2,0,1:T(8,128)(2,1)}), bf16[1,8,32,2048]{3,2,0,1:T(8,128)(2,1)}) %all-gather.2.cloned.1.call-update) | async-done | bytes 1048592 | tf_op jit(solution)/shard_map/all_gather | solution.py:56
  95.6 2.3 %copy.72 = bf16[1,8,32,2048]{3,2,1,0:T(8,128)(2,1)} copy(bf16[1,8,32,2048]{3,2,1,0:T(8,128)(2,1)} %bitcast.131) | data formatting | bytes 2097152
  (26 shorter events, 1.0 us)
Async XLA Ops:
  7.2 42.1 %copy-start = (f32[1,32,2048]{2,1,0:T(8,128)S(1)}, f32[1,32,2048]{2,1,0:T(8,128)}, u32[]{:S(2)}) copy-start(f32[1,32,2048]{2,1,0:T(8,128)} %param.8) | copy-start | bytes 786436
  7.2 3.0 %copy-start.6 = (s32[1,32]{1,0:T(1,128)S(1)}, s32[1,32]{1,0:T(1,128)}, u32[]{:S(2)}) copy-start(s32[1,32]{1,0:T(1,128)} %param.7) | copy-start | bytes 388
  7.2 3.0 %copy-start.1 = (f32[1,32]{1,0:T(1,128)S(1)}, f32[1,32]{1,0:T(1,128)}, u32[]{:S(2)}) copy-start(f32[1,32]{1,0:T(1,128)} %param.12) | copy-start | bytes 388
  7.2 63.3 %reduce-scatter.2.cloned.1.call-start = ((), (), s32[]{:S(2)}) async-start(), calls=%async_computation.6 | async-start | bytes 2359296 | tf_op jit(solution)/shard_map/reduce_scatter | solution.py:41
  10.1 8.8 %copy-start.3 = (bf16[1,32,2048]{2,1,0:T(8,128)(2,1)S(1)}, bf16[1,32,2048]{2,1,0:T(8,128)(2,1)}, u32[]{:S(2)}) copy-start(bf16[1,32,2048]{2,1,0:T(8,128)(2,1)} %param.11) | copy-start | bytes 393220
  10.1 9.5 %copy-start.2 = (f32[1,32]{1,0:T(1,128)S(1)}, f32[1,32]{1,0:T(1,128)}, u32[]{:S(2)}) copy-start(f32[1,32]{1,0:T(1,128)} %param.10) | copy-start | bytes 388
  10.1 28.2 %copy-start.4 = (bf16[1,32,2048]{2,1,0:T(8,128)(2,1)S(1)}, bf16[1,32,2048]{2,1,0:T(8,128)(2,1)}, u32[]{:S(2)}) copy-start(bf16[1,32,2048]{2,1,0:T(8,128)(2,1)} %param.9) | copy-start | bytes 393220
  11.6 14.5 %all-to-all-start.4 = ((f32[32,1,1]{2,1,0:T(1,128)}), f32[32,1,1]{2,1,0:T(1,128)S(1)}, u32[]{:S(2)}, u32[]{:S(2)}) async-start(f32[32,1,1]{2,1,0:T(1,128)} %copy.43), calls=%async_computation.5 | async-start | bytes 32768 | tf_op jit(solution)/shard_map/all_to_all | solution.py:34
  26.0 9.7 %all-to-all-start.2 = ((f32[32,1,1]{2,1,0:T(1,128)}), f32[32,1,1]{2,1,0:T(1,128)S(1)}, u32[]{:S(2)}, u32[]{:S(2)}) async-start(f32[32,1,1]{2,1,0:T(1,128)} %copy.40), calls=%async_computation.2 | async-start | bytes 32768 | tf_op jit(solution)/shard_map/all_to_all | solution.py:30
  35.7 11.0 %all-to-all-start.3 = ((bf16[32,2,1024]{2,1,0:T(2,128)(2,1)}), bf16[32,2,1024]{2,1,0:T(2,128)(2,1)S(1)}, u32[]{:S(2)}, u32[]{:S(2)}) async-start(bf16[32,2,1024]{2,1,0:T(2,128)(2,1)} %reshape.649), calls=%async_computation.4 | async-start | bytes 262144 | tf_op jit(solution)/shard_map/all_to_all | solution.py:31
  46.7 11.0 %all-to-all-start.1 = ((bf16[32,2,1024]{2,1,0:T(2,128)(2,1)}), bf16[32,2,1024]{2,1,0:T(2,128)(2,1)S(1)}, u32[]{:S(2)}, u32[]{:S(2)}) async-start(bf16[32,2,1024]{2,1,0:T(2,128)(2,1)} %reshape.647), calls=%async_computation.1 | async-start | bytes 262144 | tf_op jit(solution)/shard_map/all_to_all | solution.py:27
  57.6 12.8 %all-to-all-start = ((f32[32,1,2048]{2,1,0:T(1,128)}), f32[32,1,2048]{2,1,0:T(1,128)S(1)}, u32[]{:S(2)}, u32[]{:S(2)}) async-start(f32[32,1,2048]{2,1,0:T(1,128)} %copy.37), calls=%async_computation | async-start | bytes 524288 | tf_op jit(solution)/shard_map/all_to_all | solution.py:26
  60.2 35.3 %all-gather.2.cloned.1.call-start = ((), (), s32[]{:S(2)}) async-start(), calls=%async_computation.7 | async-start | bytes 1179648 | tf_op jit(solution)/shard_map/all_gather | solution.py:56
  70.5 3.8 %copy-start.5 = (f32[1,1,1,32,2048]{4,3,1,0,2:T(8,128)S(1)}, f32[1,1,1,32,2048]{4,3,1,0,2:T(8,128)}, u32[]{:S(2)}) copy-start(f32[1,1,1,32,2048]{4,3,1,0,2:T(8,128)} %reduce-scatter.2.cloned.1.call-done) | copy-start | bytes 786436
Sparse Core Ops, SparseCore 0:
  11.3 46.3 reduce-scatter.1
  74.1 21.3 all-gather.1
where the time goes:
time: 105 us
  waiting for transfers between devices  51.7 us (49%)
  starting transfers between devices  17.7 us (17%)
  between operations  14.2 us (14%)
  local copies, waits for them, and re-layouts  11 us (10%)
  other arithmetic  10.1 us (10%)
    all_gather x1, waiting for transfers between devices, on_device(): weights = lax.all_gather(local_weights, 'dp', axis=1, tiled=True)  19.2 us
    all_to_all x1, waiting for transfers between devices, on_device(): lax.all_to_all(shaped[0], ('dp', 'tensor'), split_axis=0, concat_axis=0,...  9.21 us
    all_to_all x1, starting transfers between devices, on_device(): lax.all_to_all(shaped[4], ('dp', 'tensor'), split_axis=0, concat_axis=0,...  7.33 us
    all_to_all x1, waiting for transfers between devices, on_device(): lax.all_to_all(shaped[1].astype(jnp.float32), ('dp', 'tensor'), split_axi...  6.73 us
    all_to_all x1, waiting for transfers between devices, on_device(): lax.all_to_all(shaped[3].astype(jnp.float32), ('dp', 'tensor'), split_axi...  6.3 us
    all_to_all x1, waiting for transfers between devices, on_device(): lax.all_to_all(shaped[2], ('dp', 'tensor'), split_axis=0, concat_axis=0,...  5.2 us
    all_to_all x1, waiting for transfers between devices, on_device(): lax.all_to_all(shaped[4], ('dp', 'tensor'), split_axis=0, concat_axis=0,...  5.05 us
    unnamed x19, local copies, waits for them, and re-layouts  4 us
  transfers between devices with their start and end apart: 7, of which 6 were waited for; matrix products, arithmetic and copies ran while one was open for 12% of the time, Pallas kernels for 0%

commit v1 on v0

--- a/solution.py
+++ b/solution.py
@@ -53,7 +53,27 @@
     new_scale_two = jnp.max(jnp.abs(moment_two), axis=1) + 1e-06
     new_code_two = (moment_two / new_scale_two[:, None]).astype(jnp.bfloat16)
     local_weights = new_master.astype(jnp.bfloat16).reshape(1, 1, slots, width)
-    weights = lax.all_gather(local_weights, "dp", axis=1, tiled=True)
+    peers, position, extent = (lax.axis_size("dp"), lax.axis_index("dp"), local_weights.shape[1])
+    ahead = [(i, (i + 1) % peers) for i in range(peers)]
+    left = [(i, (i - 1) % peers) for i in range(peers)]
+    result = jnp.zeros(
+        (*local_weights.shape[:1], peers * extent, *local_weights.shape[1 + 1 :]),
+        local_weights.dtype,
+    )
+    result = lax.dynamic_update_slice_in_dim(result, local_weights, position * extent, axis=1)
+    from_left = from_right = local_weights
+    middle = peers // 2
+    for step in range(1, middle + 1):
+        from_left = lax.ppermute(from_left, "dp", ahead)
+        result = lax.dynamic_update_slice_in_dim(
+            result, from_left, (position - step) % peers * extent, axis=1
+        )
+        if step < peers - middle:
+            from_right = lax.ppermute(from_right, "dp", left)
+            result = lax.dynamic_update_slice_in_dim(
+                result, from_right, (position + step) % peers * extent, axis=1
+            )
+    weights = result
     return (
         new_master.reshape(1, slots, width),
         new_code_one.reshape(1, slots, width),

time: 105 us -> 115 us (1.095)
  starting transfers between devices: 17.7 us -> 25.6 us
  waiting for transfers between devices: 51.7 us -> 53.6 us
  local copies, waits for them, and re-layouts: 11 us -> 9.67 us
    ppermute x0 -> x7, waiting for transfers between devices: none -> 21.5 us  [the longest x4 20.9 us: on_device(): from_left = lax.ppermute(from_left, 'dp', ahead)]
    all_gather x1 -> x0, waiting for transfers between devices: 19.2 us -> none  [on_device(): weights = lax.all_gather(local_weights, 'dp', axis=1, tiled=True)]
    ppermute x0 -> x7, starting transfers between devices: none -> 7.99 us  [the longest x3 7.59 us: on_device(): from_right = lax.ppermute(from_right, 'dp', left)]
    unnamed x19 -> x20, local copies, waits for them, and re-layouts: 4 us -> 2.66 us
  transfers between devices with their start and end apart: 7 -> 13, of which waited for: 6 -> 10; matrix products, arithmetic and copies ran while one was open for 12% -> 12% of each run, Pallas kernels for 0% -> 0%
where the time goes in v1:
time: 115 us; the launch traced here: 114 us
  waiting for transfers between devices  53.6 us (47%)
  starting transfers between devices  25.6 us (22%)
  between operations  14.4 us (13%)
  other arithmetic  11 us (10%)
  local copies, waits for them, and re-layouts  9.67 us (8%)
    ppermute x4, waiting for transfers between devices, on_device(): from_left = lax.ppermute(from_left, 'dp', ahead)  20.9 us
    all_to_all x1, waiting for transfers between devices, on_device(): lax.all_to_all(shaped[0], ('dp', 'tensor'), split_axis=0, concat_axis=0,...  8.86 us
    ppermute x3, starting transfers between devices, on_device(): from_right = lax.ppermute(from_right, 'dp', left)  7.59 us
    all_to_all x1, starting transfers between devices, on_device(): lax.all_to_all(shaped[4], ('dp', 'tensor'), split_axis=0, concat_axis=0,...  7.33 us
    all_to_all x1, waiting for transfers between devices, on_device(): lax.all_to_all(shaped[1].astype(jnp.float32), ('dp', 'tensor'), split_axi...  6.73 us
    all_to_all x1, waiting for transfers between devices, on_device(): lax.all_to_all(shaped[3].astype(jnp.float32), ('dp', 'tensor'), split_axi...  6.3 us
    all_to_all x1, waiting for transfers between devices, on_device(): lax.all_to_all(shaped[2], ('dp', 'tensor'), split_axis=0, concat_axis=0,...  5.2 us
    all_to_all x1, waiting for transfers between devices, on_device(): lax.all_to_all(shaped[4], ('dp', 'tensor'), split_axis=0, concat_axis=0,...  5.05 us
  transfers between devices with their start and end apart: 13, of which 10 were waited for; matrix products, arithmetic and copies ran while one was open for 12% of the time, Pallas kernels for 0%

profile of v1, /device:TPU:0, one launch (start us, length us, event | category | flops | bytes accessed | tf_op | source)
XLA Modules:
  0.0 114.4 jit_solution(1938217730490275275)
XLA Ops:
  7.2 2.8 %bitcast_convert_fusion = f32[1,1,8,32,2048]{4,3,1,0,2:T(8,128)} fusion(bf16[1,1,8,32,2048]{4,3,2,1,0:T(8,128)(2,1)} %param.13), kind=kLoop, calls=%fused_computation.5 | loop fusion | flops 524288 | bytes 3145728 | tf_op jit(solution)/shard_map/convert_element_type | solution.py:41
  10.2 0.7 gather_fusion.4
  10.9 0.7 copy.55
  11.6 7.3 %all-to-all-start.4 = ((f32[32,1,1]{2,1,0:T(1,128)}), f32[32,1,1]{2,1,0:T(1,128)S(1)}, u32[]{:S(2)}, u32[]{:S(2)}) async-start(f32[32,1,1]{2,1,0:T(1,128)} %copy.55), calls=%async_computation.5 | async-start | bytes 32768 | tf_op jit(solution)/shard_map/all_to_all | solution.py:34
  19.6 0.7 gather_fusion.2
  20.3 0.7 copy.52
  21.0 5.0 %all-to-all-done.4 = f32[32,1,1]{2,1,0:T(1,128)S(1)} async-done(((f32[32,1,1]{2,1,0:T(1,128)}), f32[32,1,1]{2,1,0:T(1,128)S(1)}, u32[]{:S(2)}, u32[]{:S(2)}) %all-to-all-start.4) | async-done | bytes 160 | tf_op jit(solution)/shard_map/all_to_all | solution.py:34
  26.0 2.5 %all-to-all-start.2 = ((f32[32,1,1]{2,1,0:T(1,128)}), f32[32,1,1]{2,1,0:T(1,128)S(1)}, u32[]{:S(2)}, u32[]{:S(2)}) async-start(f32[32,1,1]{2,1,0:T(1,128)} %copy.52), calls=%async_computation.2 | async-start | bytes 32768 | tf_op jit(solution)/shard_map/all_to_all | solution.py:30
  29.1 0.7 reduce.2
  29.8 0.7 reshape.649
  30.5 5.2 %all-to-all-done.2 = f32[32,1,1]{2,1,0:T(1,128)S(1)} async-done(((f32[32,1,1]{2,1,0:T(1,128)}), f32[32,1,1]{2,1,0:T(1,128)S(1)}, u32[]{:S(2)}, u32[]{:S(2)}) %all-to-all-start.2) | async-done | bytes 160 | tf_op jit(solution)/shard_map/all_to_all | solution.py:30
  35.7 2.6 %all-to-all-start.3 = ((bf16[32,2,1024]{2,1,0:T(2,128)(2,1)}), bf16[32,2,1024]{2,1,0:T(2,128)(2,1)S(1)}, u32[]{:S(2)}, u32[]{:S(2)}) async-start(bf16[32,2,1024]{2,1,0:T(2,128)(2,1)} %reshape.649), calls=%async_computation.4 | async-start | bytes 262144 | tf_op jit(solution)/shard_map/all_to_all | solution.py:31
  38.9 0.7 reduce.3
  39.6 0.7 reshape.647
  40.4 6.3 %all-to-all-done.3 = bf16[32,2,1024]{2,1,0:T(2,128)(2,1)S(1)} async-done(((bf16[32,2,1024]{2,1,0:T(2,128)(2,1)}), bf16[32,2,1024]{2,1,0:T(2,128)(2,1)S(1)}, u32[]{:S(2)}, u32[]{:S(2)}) %all-to-all-start.3) | async-done | bytes 131104 | tf_op jit(solution)/shard_map/all_to_all | solution.py:31
  46.7 2.6 %all-to-all-start.1 = ((bf16[32,2,1024]{2,1,0:T(2,128)(2,1)}), bf16[32,2,1024]{2,1,0:T(2,128)(2,1)S(1)}, u32[]{:S(2)}, u32[]{:S(2)}) async-start(bf16[32,2,1024]{2,1,0:T(2,128)(2,1)} %reshape.647), calls=%async_computation.1 | async-start | bytes 262144 | tf_op jit(solution)/shard_map/all_to_all | solution.py:27
  49.2 0.7 gather_fusion
  49.9 1.0 copy.49
  50.9 6.7 %all-to-all-done.1 = bf16[32,2,1024]{2,1,0:T(2,128)(2,1)S(1)} async-done(((bf16[32,2,1024]{2,1,0:T(2,128)(2,1)}), bf16[32,2,1024]{2,1,0:T(2,128)(2,1)S(1)}, u32[]{:S(2)}, u32[]{:S(2)}) %all-to-all-start.1) | async-done | bytes 131104 | tf_op jit(solution)/shard_map/all_to_all | solution.py:27
  57.6 2.6 %all-to-all-start = ((f32[32,1,2048]{2,1,0:T(1,128)}), f32[32,1,2048]{2,1,0:T(1,128)S(1)}, u32[]{:S(2)}, u32[]{:S(2)}) async-start(f32[32,1,2048]{2,1,0:T(1,128)} %copy.49), calls=%async_computation | async-start | bytes 524288 | tf_op jit(solution)/shard_map/all_to_all | solution.py:26
  61.6 8.9 %all-to-all-done = f32[32,1,2048]{2,1,0:T(1,128)S(1)} async-done(((f32[32,1,2048]{2,1,0:T(1,128)}), f32[32,1,2048]{2,1,0:T(1,128)S(1)}, u32[]{:S(2)}, u32[]{:S(2)}) %all-to-all-start) | async-done | bytes 262176 | tf_op jit(solution)/shard_map/all_to_all | solution.py:26
  70.4 2.8 %fusion.24 = bf16[1,1,32,2048]{3,0,2,1:T(2,128)(2,1)S(1)} fusion(f32[1,1,1,32,2048]{4,3,1,0,2:T(8,128)} %reduce-scatter.2.cloned.1.call-done, f32[1,1,32,2048]{3,2,1,0:T(8,128)S(1)} %get-tuple-element.8, f32[32,1,2048]{2,1,0:T(1,128)S(1)} %all-to-all-done, f32[32]{0:T(128)S(1)} %reduce.1, bf16[32,1,2048]{2,1,0:T(2,128)(2,1)S(1)} %reshape.650), kind=kLoop, calls=%fused_computation.50 | loop fusion | flops 1114112 | bytes 1048704 | tf_op jit(solution)/shard_map/convert_element_type | solution.py:55
  73.6 2.3 %collective-permute-start.1 = (bf16[1,1,32,2048]{3,0,2,1:T(2,128)(2,1)S(1)}, bf16[1,1,32,2048]{3,0,2,1:T(2,128)(2,1)S(1)}, u32[]{:S(2)}, u32[]{:S(2)}) collective-permute-start(bf16[1,1,32,2048]{3,0,2,1:T(2,128)(2,1)S(1)} %fusion.24), channel_id=1, source_target_pairs={{0,28},{4,0},{8,4},{12,8},{16,12},{20,16},{24,20},{28,24},{1,29},{... | collective-permute-start | bytes 393224 | tf_op jit(solution)/shard_map/ppermute | solution.py:72
  75.9 1.3 %fusion.3 = (f32[32]{0:T(128)S(1)}, f32[32]{0:T(128)S(1)}) fusion(f32[1,1,1,32,2048]{4,3,1,0,2:T(8,128)} %reduce-scatter.2.cloned.1.call-done, f32[32,1,2048]{2,1,0:T(1,128)S(1)} %convert_element_type.203, f32[32]{0:T(128)S(1)} %reduce.1, f32[32]{0:T(128)S(1)} %reduce, bf16[32,1,2048]{2,0,1:T(8,128)(2,1)S(1)} %get-tuple-element.9), kind=kLoop, calls=%fused_computation.15 | loop fusion | flops 917440 | bytes 655872 | tf_op jit(solution)/shard_map/reduce_max | solution.py:53
  77.7 1.2 %divide_convert_fusion = (bf16[1,32,2048]{2,1,0:T(8,128)(2,1)}, f32[1,32,2048]{2,1,0:T(8,128)}, bf16[1,32,2048]{2,1,0:T(8,128)(2,1)}) fusion(f32[32]{0:T(128)S(1)} %get-tuple-element.17, f32[1,1,1,32,2048]{4,3,1,0,2:T(8,128)S(1)} %copy-done.5, f32[32,1,2048]{2,1,0:T(1,128)S(1)} %convert_element_type.203, f32[32]{0:T(128)S(1)} %reduce.1, f32[32]{0:T(128)S(1)} %reduce, ...), kind=kLoop, calls=%fused_computation.47 | loop fusion | flops 1441792 | bytes 1442304 | tf_op jit(solution)/shard_map/convert_element_type | solution.py:54
  79.2 3.3 %collective-permute-done = bf16[1,1,32,2048]{3,0,2,1:T(2,128)(2,1)S(1)} collective-permute-done((bf16[1,1,32,2048]{3,0,2,1:T(2,128)(2,1)S(1)}, bf16[1,1,32,2048]{3,0,2,1:T(2,128)(2,1)S(1)}, u32[]{:S(2)}, u32[]{:S(2)}) %collective-permute-start) | collective-permute-done | bytes 131104 | tf_op jit(solution)/shard_map/ppermute | solution.py:67
  82.5 2.6 %collective-permute-start.3 = (bf16[1,1,32,2048]{3,0,2,1:T(2,128)(2,1)S(1)}, bf16[1,1,32,2048]{3,0,2,1:T(2,128)(2,1)S(1)}, u32[]{:S(2)}, u32[]{:S(2)}) collective-permute-start(bf16[1,1,32,2048]{3,0,2,1:T(2,128)(2,1)S(1)} %collective-permute-done.1), channel_id=1, source_target_pairs={{0,28},{4,0},{8,4},{12,8},{16,12},{20,16},{24,20},{28,24},{1,29},{... | collective-permute-start | bytes 393224 | tf_op jit(solution)/shard_map/ppermute | solution.py:72
  85.3 6.1 %collective-permute-done.2 = bf16[1,1,32,2048]{3,0,2,1:T(2,128)(2,1)S(1)} collective-permute-done((bf16[1,1,32,2048]{3,0,2,1:T(2,128)(2,1)S(1)}, bf16[1,1,32,2048]{3,0,2,1:T(2,128)(2,1)S(1)}, u32[]{:S(2)}, u32[]{:S(2)}) %collective-permute-start.2) | collective-permute-done | bytes 131104 | tf_op jit(solution)/shard_map/ppermute | solution.py:67
  91.4 2.6 %collective-permute-start.5 = (bf16[1,1,32,2048]{3,0,2,1:T(2,128)(2,1)S(1)}, bf16[1,1,32,2048]{3,0,2,1:T(2,128)(2,1)S(1)}, u32[]{:S(2)}, u32[]{:S(2)}) collective-permute-start(bf16[1,1,32,2048]{3,0,2,1:T(2,128)(2,1)S(1)} %collective-permute-done.3), channel_id=1, source_target_pairs={{0,28},{4,0},{8,4},{12,8},{16,12},{20,16},{24,20},{28,24},{1,29},{... | collective-permute-start | bytes 393224 | tf_op jit(solution)/shard_map/ppermute | solution.py:72
  94.2 5.5 %collective-permute-done.4 = bf16[1,1,32,2048]{3,0,2,1:T(2,128)(2,1)S(1)} collective-permute-done((bf16[1,1,32,2048]{3,0,2,1:T(2,128)(2,1)S(1)}, bf16[1,1,32,2048]{3,0,2,1:T(2,128)(2,1)S(1)}, u32[]{:S(2)}, u32[]{:S(2)}) %collective-permute-start.4) | collective-permute-done | bytes 131104 | tf_op jit(solution)/shard_map/ppermute | solution.py:67
  100.5 6.0 %collective-permute-done.6 = bf16[1,1,32,2048]{3,0,2,1:T(2,128)(2,1)S(1)} collective-permute-done((bf16[1,1,32,2048]{3,0,2,1:T(2,128)(2,1)S(1)}, bf16[1,1,32,2048]{3,0,2,1:T(2,128)(2,1)S(1)}, u32[]{:S(2)}, u32[]{:S(2)}) %collective-permute-start.6) | collective-permute-done | bytes 131104 | tf_op jit(solution)/shard_map/ppermute | solution.py:67
  106.6 1.0 copy-done.6
  (46 shorter events, 5.4 us)
Async XLA Ops:
  7.2 42.1 %copy-start = (f32[1,32,2048]{2,1,0:T(8,128)S(1)}, f32[1,32,2048]{2,1,0:T(8,128)}, u32[]{:S(2)}) copy-start(f32[1,32,2048]{2,1,0:T(8,128)} %param.8) | copy-start | bytes 786436
  7.2 2.9 %copy-start.7 = (s32[1,32]{1,0:T(1,128)S(1)}, s32[1,32]{1,0:T(1,128)}, u32[]{:S(2)}) copy-start(s32[1,32]{1,0:T(1,128)} %param.7) | copy-start | bytes 388
  7.2 3.0 %copy-start.1 = (f32[1,32]{1,0:T(1,128)S(1)}, f32[1,32]{1,0:T(1,128)}, u32[]{:S(2)}) copy-start(f32[1,32]{1,0:T(1,128)} %param.12) | copy-start | bytes 388
  7.2 63.2 %reduce-scatter.2.cloned.1.call-start = ((), (), s32[]{:S(2)}) async-start(), calls=%async_computation.6 | async-start | bytes 2359296 | tf_op jit(solution)/shard_map/reduce_scatter | solution.py:41
  10.1 8.8 %copy-start.3 = (bf16[1,32,2048]{2,1,0:T(8,128)(2,1)S(1)}, bf16[1,32,2048]{2,1,0:T(8,128)(2,1)}, u32[]{:S(2)}) copy-start(bf16[1,32,2048]{2,1,0:T(8,128)(2,1)} %param.11) | copy-start | bytes 393220
  10.1 9.5 %copy-start.2 = (f32[1,32]{1,0:T(1,128)S(1)}, f32[1,32]{1,0:T(1,128)}, u32[]{:S(2)}) copy-start(f32[1,32]{1,0:T(1,128)} %param.10) | copy-start | bytes 388
  10.1 28.2 %copy-start.4 = (bf16[1,32,2048]{2,1,0:T(8,128)(2,1)S(1)}, bf16[1,32,2048]{2,1,0:T(8,128)(2,1)}, u32[]{:S(2)}) copy-start(bf16[1,32,2048]{2,1,0:T(8,128)(2,1)} %param.9) | copy-start | bytes 393220
  11.6 14.5 %all-to-all-start.4 = ((f32[32,1,1]{2,1,0:T(1,128)}), f32[32,1,1]{2,1,0:T(1,128)S(1)}, u32[]{:S(2)}, u32[]{:S(2)}) async-start(f32[32,1,1]{2,1,0:T(1,128)} %copy.55), calls=%async_computation.5 | async-start | bytes 32768 | tf_op jit(solution)/shard_map/all_to_all | solution.py:34
  26.0 9.7 %all-to-all-start.2 = ((f32[32,1,1]{2,1,0:T(1,128)}), f32[32,1,1]{2,1,0:T(1,128)S(1)}, u32[]{:S(2)}, u32[]{:S(2)}) async-start(f32[32,1,1]{2,1,0:T(1,128)} %copy.52), calls=%async_computation.2 | async-start | bytes 32768 | tf_op jit(solution)/shard_map/all_to_all | solution.py:30
  35.7 11.0 %all-to-all-start.3 = ((bf16[32,2,1024]{2,1,0:T(2,128)(2,1)}), bf16[32,2,1024]{2,1,0:T(2,128)(2,1)S(1)}, u32[]{:S(2)}, u32[]{:S(2)}) async-start(bf16[32,2,1024]{2,1,0:T(2,128)(2,1)} %reshape.649), calls=%async_computation.4 | async-start | bytes 262144 | tf_op jit(solution)/shard_map/all_to_all | solution.py:31
  46.7 11.0 %all-to-all-start.1 = ((bf16[32,2,1024]{2,1,0:T(2,128)(2,1)}), bf16[32,2,1024]{2,1,0:T(2,128)(2,1)S(1)}, u32[]{:S(2)}, u32[]{:S(2)}) async-start(bf16[32,2,1024]{2,1,0:T(2,128)(2,1)} %reshape.647), calls=%async_computation.1 | async-start | bytes 262144 | tf_op jit(solution)/shard_map/all_to_all | solution.py:27
  57.6 12.8 %all-to-all-start = ((f32[32,1,2048]{2,1,0:T(1,128)}), f32[32,1,2048]{2,1,0:T(1,128)S(1)}, u32[]{:S(2)}, u32[]{:S(2)}) async-start(f32[32,1,2048]{2,1,0:T(1,128)} %copy.49), calls=%async_computation | async-start | bytes 524288 | tf_op jit(solution)/shard_map/all_to_all | solution.py:26
  70.4 7.3 %copy-start.5 = (f32[1,1,1,32,2048]{4,3,1,0,2:T(8,128)S(1)}, f32[1,1,1,32,2048]{4,3,1,0,2:T(8,128)}, u32[]{:S(2)}) copy-start(f32[1,1,1,32,2048]{4,3,1,0,2:T(8,128)} %reduce-scatter.2.cloned.1.call-done) | copy-start | bytes 786436
  73.2 9.2 %collective-permute-start = (bf16[1,1,32,2048]{3,0,2,1:T(2,128)(2,1)S(1)}, bf16[1,1,32,2048]{3,0,2,1:T(2,128)(2,1)S(1)}, u32[]{:S(2)}, u32[]{:S(2)}) collective-permute-start(bf16[1,1,32,2048]{3,0,2,1:T(2,128)(2,1)S(1)} %fusion.24), channel_id=1, source_target_pairs={{0,4},{4,8},{8,12},{12,16},{16,20},{20,24},{24,28},{28,0},{1,5},{5... | collective-permute-start | bytes 393224 | tf_op jit(solution)/shard_map/ppermute | solution.py:67
  73.6 8.8 %collective-permute-start.1 = (bf16[1,1,32,2048]{3,0,2,1:T(2,128)(2,1)S(1)}, bf16[1,1,32,2048]{3,0,2,1:T(2,128)(2,1)S(1)}, u32[]{:S(2)}, u32[]{:S(2)}) collective-permute-start(bf16[1,1,32,2048]{3,0,2,1:T(2,128)(2,1)S(1)} %fusion.24), channel_id=1, source_target_pairs={{0,28},{4,0},{8,4},{12,8},{16,12},{20,16},{24,20},{28,24},{1,29},{... | collective-permute-start | bytes 393224 | tf_op jit(solution)/shard_map/ppermute | solution.py:72
  82.4 9.0 %collective-permute-start.2 = (bf16[1,1,32,2048]{3,0,2,1:T(2,128)(2,1)S(1)}, bf16[1,1,32,2048]{3,0,2,1:T(2,128)(2,1)S(1)}, u32[]{:S(2)}, u32[]{:S(2)}) collective-permute-start(bf16[1,1,32,2048]{3,0,2,1:T(2,128)(2,1)S(1)} %collective-permute-done), channel_id=1, source_target_pairs={{0,4},{4,8},{8,12},{12,16},{16,20},{20,24},{24,28},{28,0},{1,5},{5... | collective-permute-start | bytes 393224 | tf_op jit(solution)/shard_map/ppermute | solution.py:67
  82.5 9.0 %collective-permute-start.3 = (bf16[1,1,32,2048]{3,0,2,1:T(2,128)(2,1)S(1)}, bf16[1,1,32,2048]{3,0,2,1:T(2,128)(2,1)S(1)}, u32[]{:S(2)}, u32[]{:S(2)}) collective-permute-start(bf16[1,1,32,2048]{3,0,2,1:T(2,128)(2,1)S(1)} %collective-permute-done.1), channel_id=1, source_target_pairs={{0,28},{4,0},{8,4},{12,8},{16,12},{20,16},{24,20},{28,24},{1,29},{... | collective-permute-start | bytes 393224 | tf_op jit(solution)/shard_map/ppermute | solution.py:72
  91.4 8.4 %collective-permute-start.4 = (bf16[1,1,32,2048]{3,0,2,1:T(2,128)(2,1)S(1)}, bf16[1,1,32,2048]{3,0,2,1:T(2,128)(2,1)S(1)}, u32[]{:S(2)}, u32[]{:S(2)}) collective-permute-start(bf16[1,1,32,2048]{3,0,2,1:T(2,128)(2,1)S(1)} %collective-permute-done.2), channel_id=1, source_target_pairs={{0,4},{4,8},{8,12},{12,16},{16,20},{20,24},{24,28},{28,0},{1,5},{5... | collective-permute-start | bytes 393224 | tf_op jit(solution)/shard_map/ppermute | solution.py:67
  91.4 9.0 %collective-permute-start.5 = (bf16[1,1,32,2048]{3,0,2,1:T(2,128)(2,1)S(1)}, bf16[1,1,32,2048]{3,0,2,1:T(2,128)(2,1)S(1)}, u32[]{:S(2)}, u32[]{:S(2)}) collective-permute-start(bf16[1,1,32,2048]{3,0,2,1:T(2,128)(2,1)S(1)} %collective-permute-done.3), channel_id=1, source_target_pairs={{0,28},{4,0},{8,4},{12,8},{16,12},{20,16},{24,20},{28,24},{1,29},{... | collective-permute-start | bytes 393224 | tf_op jit(solution)/shard_map/ppermute | solution.py:72
  99.8 6.7 %collective-permute-start.6 = (bf16[1,1,32,2048]{3,0,2,1:T(2,128)(2,1)S(1)}, bf16[1,1,32,2048]{3,0,2,1:T(2,128)(2,1)S(1)}, u32[]{:S(2)}, u32[]{:S(2)}) collective-permute-start(bf16[1,1,32,2048]{3,0,2,1:T(2,128)(2,1)S(1)} %collective-permute-done.4), channel_id=1, source_target_pairs={{0,4},{4,8},{8,12},{12,16},{16,20},{20,24},{24,28},{28,0},{1,5},{5... | collective-permute-start | bytes 393224 | tf_op jit(solution)/shard_map/ppermute | solution.py:67
  106.5 1.0 copy-start.6
Sparse Core Ops, SparseCore 0:
  11.3 46.3 reduce-scatter.1
